TPU v7x, 1024 devices: a whole 4x8x16 slice. The times are simulated.
1024 devices in a mesh: section: 16 (over z_hi, x), dp: 64 (over z_lo, y, core).
Axes of the slice: x: 4, y: 8, z: 16 (z_hi: 4, z_lo: 4; z = z_hi * 4 + z_lo), core: 2. Of those that a mesh axis runs over, the one named last changes fastest.
Arguments:
- fresh_q: bfloat16 [16, 7168, 2048], P('section', 'dp'), may hold values from -6 to 6
- current_key_value: bfloat16 [16, 7168, 512], P('section', 'dp'), may hold values from -6 to 6
- held_q: bfloat16 [16, 7168, 2048], P('section', 'dp'), may hold values from -6 to 6
- retained_key_value: bfloat16 [16, 7168, 512], P('section', 'dp'), may hold values from -6 to 6
- cotangent: bfloat16 [16, 7168, 2048], P('section', 'dp'), may hold values from -6 to 6
- norm_gains: float32 [16, 2, 128], P('section'), may hold values from 0.5 to 1.5
- plan: int32 [16, 2], P('section'), may hold values from 0 to 15, as said below
- segment_ids: int32 [64, 16, 112], P('dp'), may hold values from 0 to 3, never falling along the last dimension, each value on 1 to 56 neighbouring positions
Outputs:
- attention_out: bfloat16 [16, 7168, 2048], P('section', 'dp')
- stored_q: bfloat16 [16, 7168, 2048], P('section', 'dp')
- stored_kv: bfloat16 [16, 7168, 512], P('section', 'dp')
- grad_q: bfloat16 [16, 7168, 2048], P('section', 'dp')
- key_value_gradient: bfloat16 [16, 7168, 512], P('section', 'dp')
- gain_grads: float32 [16, 2, 128], P('section')
Inputs may be any that keep to these rules, and one draw needn't show every extreme that they name: `plan`: each of the two columns holds every microbatch number 0 to 15 exactly once.
All inputs are finite; a program needn't handle non-finite values.
Results may differ from a plain program's by a relative error of at most 0.0065.
Values may be sent and summed in bfloat16 or wider, within the bound.
A program may use at most 32 MiB of HBM per device.

v0:
```python
import math

import jax
import jax.numpy as jnp
from jax import lax
from jax.sharding import PartitionSpec as P

HQ = 16
KV_HEAD_COUNT = 2
HEAD_SIZE = 128
QUERY_PER_KV = 8


EPSILON = 1e-06


def partner(value, axis, distance):
    mask = 2**distance
    pairs = [(source, source ^ mask) for source in range(lax.axis_size(axis))]
    return lax.ppermute(value, axis, pairs)


def shifted(block, axis, distance):
    devices = range(lax.axis_size(axis))
    route = [((i - distance) % len(devices), i) for i in devices]
    return lax.ppermute(block, axis, route)


def allowed_pairs(segment_row):
    row_sum_total = segment_row.shape[0]
    rows_at = jnp.arange(row_sum_total)[:, None]
    cols_at = jnp.arange(row_sum_total)[None, :]
    return (cols_at <= rows_at) & (segment_row[:, None] == segment_row[None, :])


def apply_norm(values, gain, heads):
    row_sum_total = values.shape[0]
    widened = values.astype(jnp.float32).reshape(row_sum_total, heads, HEAD_SIZE)
    factor = lax.rsqrt(jnp.mean(widened * widened, axis=-1, keepdims=True) + EPSILON)
    return (widened, factor, widened * factor * gain)


def attention_probs(query_rows, key_value_pair, gain_per_row, segment_row):
    row_sum_total = query_rows.shape[0]
    q_wide, q_factor, normalized_query = apply_norm(query_rows, gain_per_row[0], HQ)
    expanded_key, key_factor, normalized_key = apply_norm(
        key_value_pair[:, : KV_HEAD_COUNT * HEAD_SIZE], gain_per_row[1], KV_HEAD_COUNT
    )
    query_converted = normalized_query.astype(jnp.bfloat16).reshape(
        row_sum_total, KV_HEAD_COUNT, QUERY_PER_KV, HEAD_SIZE
    )
    k_cast = normalized_key.astype(jnp.bfloat16)
    scores = jnp.einsum(
        "qhgd,khd->hgqk", query_converted, k_cast, preferred_element_type=jnp.float32
    ) * (1.0 / math.sqrt(HEAD_SIZE))
    weights = jnp.where(allowed_pairs(segment_row), jnp.exp(scores), 0.0)
    attn_probs = weights / jnp.sum(weights, axis=-1, keepdims=True)
    return (q_wide, q_factor, query_converted, expanded_key, key_factor, k_cast, attn_probs)


def forward(query_rows, key_value_pair, gain_per_row, segment_row):
    row_sum_total = query_rows.shape[0]
    attn_probs = attention_probs(query_rows, key_value_pair, gain_per_row, segment_row)[6]
    value_portion = key_value_pair[:, KV_HEAD_COUNT * HEAD_SIZE :].reshape(
        row_sum_total, KV_HEAD_COUNT, HEAD_SIZE
    )
    output = jnp.einsum(
        "hgqk,khd->qhgd",
        attn_probs.astype(jnp.bfloat16),
        value_portion,
        preferred_element_type=jnp.float32,
    )
    return output.reshape(row_sum_total, HQ * HEAD_SIZE).astype(jnp.bfloat16)


def norm_back(widened, factor, gain, d_normed):
    scaled = gain * d_normed
    inner = jnp.sum(widened * scaled, axis=-1, keepdims=True) / HEAD_SIZE
    d_input = factor * scaled - widened * factor * factor * factor * inner
    d_gain = jnp.sum(d_normed * widened * factor, axis=(0, 1))
    return (d_input, d_gain)


def backward(query_rows, key_value_pair, gain_per_row, segment_row, received_payload):
    row_sum_total = query_rows.shape[0]
    q_wide, q_factor, query_converted, expanded_key, key_factor, k_cast, attn_probs = (
        attention_probs(query_rows, key_value_pair, gain_per_row, segment_row)
    )
    value_portion = key_value_pair[:, KV_HEAD_COUNT * HEAD_SIZE :].reshape(
        row_sum_total, KV_HEAD_COUNT, HEAD_SIZE
    )
    expanded_heads = received_payload.reshape(row_sum_total, KV_HEAD_COUNT, QUERY_PER_KV, HEAD_SIZE)
    prob_cast = attn_probs.astype(jnp.bfloat16)
    d_probs = jnp.einsum(
        "qhgd,khd->hgqk", expanded_heads, value_portion, preferred_element_type=jnp.float32
    )
    value_gradient = jnp.einsum(
        "hgqk,qhgd->khd", prob_cast, expanded_heads, preferred_element_type=jnp.float32
    )
    centre = jnp.sum(attn_probs * d_probs, axis=-1, keepdims=True)
    d_scores = (attn_probs * (d_probs - centre)).astype(jnp.bfloat16)
    score_scale = 1.0 / math.sqrt(HEAD_SIZE)
    d_qn = (
        jnp.einsum("hgqk,khd->qhgd", d_scores, k_cast, preferred_element_type=jnp.float32).reshape(
            row_sum_total, HQ, HEAD_SIZE
        )
        * score_scale
    )
    d_kn = (
        jnp.einsum("hgqk,qhgd->khd", d_scores, query_converted, preferred_element_type=jnp.float32)
        * score_scale
    )
    grad_query, q_gain = norm_back(q_wide, q_factor, gain_per_row[0], d_qn)
    key_gradient, k_gain = norm_back(expanded_key, key_factor, gain_per_row[1], d_kn)
    grad_q = grad_query.reshape(row_sum_total, HQ * HEAD_SIZE).astype(jnp.bfloat16)
    key_value_gradient = jnp.concatenate(
        [
            key_gradient.reshape(row_sum_total, KV_HEAD_COUNT * HEAD_SIZE),
            value_gradient.reshape(row_sum_total, KV_HEAD_COUNT * HEAD_SIZE),
        ],
        axis=1,
    ).astype(jnp.bfloat16)
    return (grad_q, key_value_gradient, jnp.stack([q_gain, k_gain]))


def ascend(first, second, third, fourth, quantize_levels):
    for bit_number in range(quantize_levels):
        first, second, third, fourth = partner(
            (first, second, third, fourth), "section", bit_number
        )
    return (first, second, third, fourth)


def local(
    fresh_q, current_key_value, held_q, retained_key_value, cotangent, norm_gains, plan, segment_ids
):
    quantize_levels = lax.axis_size("section").bit_length() - 1
    gain_per_row = norm_gains[0]
    id_table = segment_ids[0]
    forward_ids = lax.dynamic_index_in_dim(id_table, plan[0, 0], 0, keepdims=False)
    backward_ids = lax.dynamic_index_in_dim(id_table, plan[0, 1], 0, keepdims=False)
    arrived = ascend(fresh_q, current_key_value, held_q, retained_key_value, quantize_levels)
    forward_out = forward(fresh_q[0], current_key_value[0], gain_per_row, forward_ids)
    attention_out = shifted(forward_out[None], "section", 1)
    upstream = shifted(cotangent, "section", -1)
    grad_q, key_value_gradient, gain_terms = backward(
        arrived[2][0], arrived[3][0], gain_per_row, backward_ids, upstream[0]
    )
    gain_total = lax.psum(gain_terms, "dp") / lax.axis_size("dp")
    return (
        attention_out,
        arrived[0],
        arrived[1],
        grad_q[None],
        key_value_gradient[None],
        gain_total[None],
    )


def solution(mesh):
    placed = (
        P("section", "dp", None),
        P("section", "dp", None),
        P("section", "dp", None),
        P("section", "dp", None),
        P("section", "dp", None),
        P("section", None, None),
        P("section", None),
        P("dp", None, None),
    )
    return jax.shard_map(
        local,
        mesh=mesh,
        in_specs=placed,
        out_specs=(
            P("section", "dp", None),
            P("section", "dp", None),
            P("section", "dp", None),
            P("section", "dp", None),
            P("section", "dp", None),
            P("section", None, None),
        ),
        check_vma=False,
    )
```

profile of v0, /device:TPU:262, one launch (start us, length us, event | category | flops | bytes accessed | tf_op | source)
XLA Modules:
  0.0 485.4 jit_solution(1063353038723714237)
XLA Ops:
  0.6 2.7 collective-permute-start.9
  3.4 3.1 collective-permute-start.13
  6.5 2.7 collective-permute-start.17
  9.2 2.4 collective-permute-start.1
  11.7 3.4 collective-permute-start.5
  15.1 1.3 fusion.52
  24.8 3.1 collective-permute-start.10
  28.6 4.3 collective-permute-start.14
  32.8 6.3 %collective-permute-done.5 = bf16[1,112,512]{2,1,0:T(8,128)(2,1)} collective-permute-done((bf16[1,112,512]{2,1,0:T(8,128)(2,1)}, bf16[1,112,512]{2,1,0:T(8,128)(2,1)}, u32[]{:S(2)}, u32[]{:S(2)}) %collective-permute-start.5) | collective-permute-done | bytes 114720 | tf_op jit(solution)/shard_map/ppermute | solution.py:20
  39.2 3.0 collective-permute-start.6
  42.3 14.3 %collective-permute-done.14 = bf16[1,112,512]{2,1,0:T(8,128)(2,1)S(1)} collective-permute-done((bf16[1,112,512]{2,1,0:T(8,128)(2,1)S(1)}, bf16[1,112,512]{2,1,0:T(8,128)(2,1)S(1)}, u32[]{:S(2)}, u32[]{:S(2)}) %collective-permute-start.14) | collective-permute-done | bytes 114720 | tf_op jit(solution)/shard_map/ppermute | solution.py:20
  56.6 4.8 collective-permute-start.15
  61.4 4.9 %collective-permute-start.7 = (bf16[1,112,512]{2,1,0:T(8,128)(2,1)S(1)}, bf16[1,112,512]{2,1,0:T(8,128)(2,1)S(1)}, u32[]{:S(2)}, u32[]{:S(2)}) collective-permute-start(bf16[1,112,512]{2,1,0:T(8,128)(2,1)S(1)} %collective-permute-done.6), channel_id=1, source_target_pairs={{0,256},{64,320},{128,384},{192,448},{256,0},{320,64},{384,128},{4... | collective-permute-start | bytes 344072 | tf_op jit(solution)/shard_map/ppermute | solution.py:20
  66.4 9.4 %collective-permute-done.15 = bf16[1,112,512]{2,1,0:T(8,128)(2,1)S(1)} collective-permute-done((bf16[1,112,512]{2,1,0:T(8,128)(2,1)S(1)}, bf16[1,112,512]{2,1,0:T(8,128)(2,1)S(1)}, u32[]{:S(2)}, u32[]{:S(2)}) %collective-permute-start.15) | collective-permute-done | bytes 114720 | tf_op jit(solution)/shard_map/ppermute | solution.py:20
  75.8 9.5 %collective-permute-start = (bf16[1,112,2048]{2,1,0:T(8,128)(2,1)S(1)}, bf16[1,112,2048]{2,1,0:T(8,128)(2,1)S(1)}, u32[]{:S(2)}, u32[]{:S(2)}) collective-permute-start(bf16[1,112,2048]{2,1,0:T(8,128)(2,1)S(1)} %convert_element_type.102), channel_id=1, source_target_pairs={{960,0},{0,64},{64,128},{128,192},{192,256},{256,320},{320,384},{3... | collective-permute-start | bytes 1376264 | tf_op jit(solution)/shard_map/ppermute | solution.py:26
  85.3 7.2 %collective-permute-start.16 = (bf16[1,112,512]{2,1,0:T(8,128)(2,1)S(1)}, bf16[1,112,512]{2,1,0:T(8,128)(2,1)S(1)}, u32[]{:S(2)}, u32[]{:S(2)}) collective-permute-start(bf16[1,112,512]{2,1,0:T(8,128)(2,1)S(1)} %collective-permute-done.15), channel_id=1, source_target_pairs={{0,512},{64,576},{128,640},{192,704},{256,768},{320,832},{384,896}... | collective-permute-start | bytes 344072 | tf_op jit(solution)/shard_map/ppermute | solution.py:20
  92.6 4.1 collective-permute-start.2
  96.7 8.5 %collective-permute-start.11 = (bf16[1,112,2048]{2,1,0:T(8,128)(2,1)S(1)}, bf16[1,112,2048]{2,1,0:T(8,128)(2,1)}, u32[]{:S(2)}, u32[]{:S(2)}) collective-permute-start(bf16[1,112,2048]{2,1,0:T(8,128)(2,1)S(1)} %collective-permute-done.10), channel_id=1, source_target_pairs={{0,256},{64,320},{128,384},{192,448},{256,0},{320,64},{384,128},{4... | collective-permute-start | bytes 1376264 | tf_op jit(solution)/shard_map/ppermute | solution.py:20
  105.2 23.5 %collective-permute-done.16 = bf16[1,112,512]{2,1,0:T(8,128)(2,1)S(1)} collective-permute-done((bf16[1,112,512]{2,1,0:T(8,128)(2,1)S(1)}, bf16[1,112,512]{2,1,0:T(8,128)(2,1)S(1)}, u32[]{:S(2)}, u32[]{:S(2)}) %collective-permute-start.16) | collective-permute-done | bytes 114720 | tf_op jit(solution)/shard_map/ppermute | solution.py:20
  128.7 3.4 collective-permute-start.8
  133.7 61.4 %collective-permute-done.8 = bf16[1,112,512]{2,1,0:T(8,128)(2,1)S(1)} collective-permute-done((bf16[1,112,512]{2,1,0:T(8,128)(2,1)S(1)}, bf16[1,112,512]{2,1,0:T(8,128)(2,1)S(1)}, u32[]{:S(2)}, u32[]{:S(2)}) %collective-permute-start.8) | collective-permute-done | bytes 114720 | tf_op jit(solution)/shard_map/ppermute | solution.py:20
  195.1 1.9 collective-permute-start.3
  197.0 1.9 collective-permute-start.12
  199.4 30.4 %collective-permute-done.3 = bf16[1,112,2048]{2,1,0:T(8,128)(2,1)} collective-permute-done((bf16[1,112,2048]{2,1,0:T(8,128)(2,1)}, bf16[1,112,2048]{2,1,0:T(8,128)(2,1)}, u32[]{:S(2)}, u32[]{:S(2)}) %collective-permute-start.3) | collective-permute-done | bytes 458784 | tf_op jit(solution)/shard_map/ppermute | solution.py:20
  229.8 6.5 %collective-permute-start.4 = (bf16[1,112,2048]{2,1,0:T(8,128)(2,1)}, bf16[1,112,2048]{2,1,0:T(8,128)(2,1)}, u32[]{:S(2)}, u32[]{:S(2)}) collective-permute-start(bf16[1,112,2048]{2,1,0:T(8,128)(2,1)} %collective-permute-done.3), channel_id=1, source_target_pairs={{0,512},{64,576},{128,640},{192,704},{256,768},{320,832},{384,896}... | collective-permute-start | bytes 1376264 | tf_op jit(solution)/shard_map/ppermute | solution.py:20
  237.0 1.6 fusion.2
  238.6 1.8 fusion.8
  240.4 1.7 multiply_reduce_fusion.1
  245.7 1.3 mul.295
  247.0 1.3 mul.296
  248.3 231.6 %psum.7 = f32[2,128]{1,0:T(2,128)S(1)} all-reduce(f32[2,128]{1,0:T(2,128)S(1)} %pad_maximum_fusion.1), channel_id=1, replica_groups=mesh['section'=16,'dp'=64] {'dp'}, use_global_device_ids=true, to_apply=%region_11.12 | all-reduce | flops 256 | bytes 2048 | tf_op jit(solution)/shard_map/psum | solution.py:149
  483.0 1.8 copy.219
  (82 shorter events, 15.0 us)
Async XLA Ops:
  0.6 24.1 %collective-permute-start.9 = (bf16[1,112,2048]{2,1,0:T(8,128)(2,1)}, bf16[1,112,2048]{2,1,0:T(8,128)(2,1)}, u32[]{:S(2)}, u32[]{:S(2)}) collective-permute-start(bf16[1,112,2048]{2,1,0:T(8,128)(2,1)} %param.10), channel_id=1, source_target_pairs={{0,64},{64,0},{128,192},{192,128},{256,320},{320,256},{384,448},{4... | collective-permute-start | bytes 1376264 | tf_op jit(solution)/shard_map/ppermute | solution.py:20
  3.4 25.2 %collective-permute-start.13 = (bf16[1,112,512]{2,1,0:T(8,128)(2,1)}, bf16[1,112,512]{2,1,0:T(8,128)(2,1)S(1)}, u32[]{:S(2)}, u32[]{:S(2)}) collective-permute-start(bf16[1,112,512]{2,1,0:T(8,128)(2,1)} %param.11), channel_id=1, source_target_pairs={{0,64},{64,0},{128,192},{192,128},{256,320},{320,256},{384,448},{4... | collective-permute-start | bytes 344072 | tf_op jit(solution)/shard_map/ppermute | solution.py:20
  6.5 126.0 %collective-permute-start.17 = (bf16[1,112,2048]{2,1,0:T(8,128)(2,1)}, bf16[1,112,2048]{2,1,0:T(8,128)(2,1)}, u32[]{:S(2)}, u32[]{:S(2)}) collective-permute-start(bf16[1,112,2048]{2,1,0:T(8,128)(2,1)} %param.12), channel_id=1, source_target_pairs={{64,0},{128,64},{192,128},{256,192},{320,256},{384,320},{448,384},... | collective-permute-start | bytes 1376264 | tf_op jit(solution)/shard_map/ppermute | solution.py:26
  9.2 83.3 %collective-permute-start.1 = (bf16[1,112,2048]{2,1,0:T(8,128)(2,1)}, bf16[1,112,2048]{2,1,0:T(8,128)(2,1)}, u32[]{:S(2)}, u32[]{:S(2)}) collective-permute-start(bf16[1,112,2048]{2,1,0:T(8,128)(2,1)} %param.8), channel_id=1, source_target_pairs={{0,64},{64,0},{128,192},{192,128},{256,320},{320,256},{384,448},{4... | collective-permute-start | bytes 1376264 | tf_op jit(solution)/shard_map/ppermute | solution.py:20
  11.7 27.5 %collective-permute-start.5 = (bf16[1,112,512]{2,1,0:T(8,128)(2,1)}, bf16[1,112,512]{2,1,0:T(8,128)(2,1)}, u32[]{:S(2)}, u32[]{:S(2)}) collective-permute-start(bf16[1,112,512]{2,1,0:T(8,128)(2,1)} %param.9), channel_id=1, source_target_pairs={{0,64},{64,0},{128,192},{192,128},{256,320},{320,256},{384,448},{4... | collective-permute-start | bytes 344072 | tf_op jit(solution)/shard_map/ppermute | solution.py:20
  19.0 1.2 copy-start
  20.2 0.7 copy-start.4
  20.2 2.8 copy-start.3
  24.8 71.9 %collective-permute-start.10 = (bf16[1,112,2048]{2,1,0:T(8,128)(2,1)}, bf16[1,112,2048]{2,1,0:T(8,128)(2,1)S(1)}, u32[]{:S(2)}, u32[]{:S(2)}) collective-permute-start(bf16[1,112,2048]{2,1,0:T(8,128)(2,1)} %collective-permute-done.9), channel_id=1, source_target_pairs={{0,128},{64,192},{128,0},{192,64},{256,384},{320,448},{384,256},{4... | collective-permute-start | bytes 1376264 | tf_op jit(solution)/shard_map/ppermute | solution.py:20
  28.6 28.0 %collective-permute-start.14 = (bf16[1,112,512]{2,1,0:T(8,128)(2,1)S(1)}, bf16[1,112,512]{2,1,0:T(8,128)(2,1)S(1)}, u32[]{:S(2)}, u32[]{:S(2)}) collective-permute-start(bf16[1,112,512]{2,1,0:T(8,128)(2,1)S(1)} %collective-permute-done.13), channel_id=1, source_target_pairs={{0,128},{64,192},{128,0},{192,64},{256,384},{320,448},{384,256},{4... | collective-permute-start | bytes 344072 | tf_op jit(solution)/shard_map/ppermute | solution.py:20
  39.2 22.3 %collective-permute-start.6 = (bf16[1,112,512]{2,1,0:T(8,128)(2,1)}, bf16[1,112,512]{2,1,0:T(8,128)(2,1)S(1)}, u32[]{:S(2)}, u32[]{:S(2)}) collective-permute-start(bf16[1,112,512]{2,1,0:T(8,128)(2,1)} %collective-permute-done.5), channel_id=1, source_target_pairs={{0,128},{64,192},{128,0},{192,64},{256,384},{320,448},{384,256},{4... | collective-permute-start | bytes 344072 | tf_op jit(solution)/shard_map/ppermute | solution.py:20
  56.6 19.2 %collective-permute-start.15 = (bf16[1,112,512]{2,1,0:T(8,128)(2,1)S(1)}, bf16[1,112,512]{2,1,0:T(8,128)(2,1)S(1)}, u32[]{:S(2)}, u32[]{:S(2)}) collective-permute-start(bf16[1,112,512]{2,1,0:T(8,128)(2,1)S(1)} %collective-permute-done.14), channel_id=1, source_target_pairs={{0,256},{64,320},{128,384},{192,448},{256,0},{320,64},{384,128},{4... | collective-permute-start | bytes 344072 | tf_op jit(solution)/shard_map/ppermute | solution.py:20
  61.4 23.9 %collective-permute-start.7 = (bf16[1,112,512]{2,1,0:T(8,128)(2,1)S(1)}, bf16[1,112,512]{2,1,0:T(8,128)(2,1)S(1)}, u32[]{:S(2)}, u32[]{:S(2)}) collective-permute-start(bf16[1,112,512]{2,1,0:T(8,128)(2,1)S(1)} %collective-permute-done.6), channel_id=1, source_target_pairs={{0,256},{64,320},{128,384},{192,448},{256,0},{320,64},{384,128},{4... | collective-permute-start | bytes 344072 | tf_op jit(solution)/shard_map/ppermute | solution.py:20
  75.8 57.8 %collective-permute-start = (bf16[1,112,2048]{2,1,0:T(8,128)(2,1)S(1)}, bf16[1,112,2048]{2,1,0:T(8,128)(2,1)S(1)}, u32[]{:S(2)}, u32[]{:S(2)}) collective-permute-start(bf16[1,112,2048]{2,1,0:T(8,128)(2,1)S(1)} %convert_element_type.102), channel_id=1, source_target_pairs={{960,0},{0,64},{64,128},{128,192},{192,256},{256,320},{320,384},{3... | collective-permute-start | bytes 1376264 | tf_op jit(solution)/shard_map/ppermute | solution.py:26
  85.3 43.4 %collective-permute-start.16 = (bf16[1,112,512]{2,1,0:T(8,128)(2,1)S(1)}, bf16[1,112,512]{2,1,0:T(8,128)(2,1)S(1)}, u32[]{:S(2)}, u32[]{:S(2)}) collective-permute-start(bf16[1,112,512]{2,1,0:T(8,128)(2,1)S(1)} %collective-permute-done.15), channel_id=1, source_target_pairs={{0,512},{64,576},{128,640},{192,704},{256,768},{320,832},{384,896}... | collective-permute-start | bytes 344072 | tf_op jit(solution)/shard_map/ppermute | solution.py:20
  92.6 102.5 %collective-permute-start.2 = (bf16[1,112,2048]{2,1,0:T(8,128)(2,1)}, bf16[1,112,2048]{2,1,0:T(8,128)(2,1)}, u32[]{:S(2)}, u32[]{:S(2)}) collective-permute-start(bf16[1,112,2048]{2,1,0:T(8,128)(2,1)} %collective-permute-done.1), channel_id=1, source_target_pairs={{0,128},{64,192},{128,0},{192,64},{256,384},{320,448},{384,256},{4... | collective-permute-start | bytes 1376264 | tf_op jit(solution)/shard_map/ppermute | solution.py:20
  96.7 100.3 %collective-permute-start.11 = (bf16[1,112,2048]{2,1,0:T(8,128)(2,1)S(1)}, bf16[1,112,2048]{2,1,0:T(8,128)(2,1)}, u32[]{:S(2)}, u32[]{:S(2)}) collective-permute-start(bf16[1,112,2048]{2,1,0:T(8,128)(2,1)S(1)} %collective-permute-done.10), channel_id=1, source_target_pairs={{0,256},{64,320},{128,384},{192,448},{256,0},{320,64},{384,128},{4... | collective-permute-start | bytes 1376264 | tf_op jit(solution)/shard_map/ppermute | solution.py:20
  128.7 66.3 %collective-permute-start.8 = (bf16[1,112,512]{2,1,0:T(8,128)(2,1)S(1)}, bf16[1,112,512]{2,1,0:T(8,128)(2,1)S(1)}, u32[]{:S(2)}, u32[]{:S(2)}) collective-permute-start(bf16[1,112,512]{2,1,0:T(8,128)(2,1)S(1)} %collective-permute-done.7), channel_id=1, source_target_pairs={{0,512},{64,576},{128,640},{192,704},{256,768},{320,832},{384,896}... | collective-permute-start | bytes 344072 | tf_op jit(solution)/shard_map/ppermute | solution.py:20
  133.6 65.8 %copy-start.1 = (bf16[1,112,2048]{2,1,0:T(8,128)(2,1)}, bf16[1,112,2048]{2,1,0:T(8,128)(2,1)S(1)}, u32[]{:S(2)}) copy-start(bf16[1,112,2048]{2,1,0:T(8,128)(2,1)S(1)} %collective-permute-done) | copy-start | bytes 1376260
  195.1 34.7 %collective-permute-start.3 = (bf16[1,112,2048]{2,1,0:T(8,128)(2,1)}, bf16[1,112,2048]{2,1,0:T(8,128)(2,1)}, u32[]{:S(2)}, u32[]{:S(2)}) collective-permute-start(bf16[1,112,2048]{2,1,0:T(8,128)(2,1)} %collective-permute-done.2), channel_id=1, source_target_pairs={{0,256},{64,320},{128,384},{192,448},{256,0},{320,64},{384,128},{4... | collective-permute-start | bytes 1376264 | tf_op jit(solution)/shard_map/ppermute | solution.py:20
  197.0 39.3 %collective-permute-start.12 = (bf16[1,112,2048]{2,1,0:T(8,128)(2,1)}, bf16[1,112,2048]{2,1,0:T(8,128)(2,1)S(1)}, u32[]{:S(2)}, u32[]{:S(2)}) collective-permute-start(bf16[1,112,2048]{2,1,0:T(8,128)(2,1)} %collective-permute-done.11), channel_id=1, source_target_pairs={{0,512},{64,576},{128,640},{192,704},{256,768},{320,832},{384,896}... | collective-permute-start | bytes 1376264 | tf_op jit(solution)/shard_map/ppermute | solution.py:20
  229.8 251.3 %collective-permute-start.4 = (bf16[1,112,2048]{2,1,0:T(8,128)(2,1)}, bf16[1,112,2048]{2,1,0:T(8,128)(2,1)}, u32[]{:S(2)}, u32[]{:S(2)}) collective-permute-start(bf16[1,112,2048]{2,1,0:T(8,128)(2,1)} %collective-permute-done.3), channel_id=1, source_target_pairs={{0,512},{64,576},{128,640},{192,704},{256,768},{320,832},{384,896}... | collective-permute-start | bytes 1376264 | tf_op jit(solution)/shard_map/ppermute | solution.py:20
  481.1 1.1 copy-start.2
where the time goes:
time: 486 us; the launch traced here: 485 us
  blocking collectives  232 us (48%)
  waiting for transfers between devices  145 us (30%)
  starting transfers between devices  77.6 us (16%)
  local copies, waits for them, and re-layouts  12.1 us (2%)
  other arithmetic  7.15 us (1%)
  matrix products  6.47 us (1%)
  between operations  5.12 us (1%)
    psum x1, blocking collectives, local(): gain_total = lax.psum(gain_terms, 'dp') / lax.axis_size('dp')  232 us
    ppermute x16, waiting for transfers between devices, partner(): return lax.ppermute(value, axis, pairs)  145 us
    ppermute x16, starting transfers between devices, partner(): return lax.ppermute(value, axis, pairs)  65.3 us
    ppermute x2, starting transfers between devices, shifted(): return lax.ppermute(block, axis, route)  12.2 us
  transfers between devices with their start and end apart: 18, of which 6 were waited for; matrix products, arithmetic and copies ran while one was open for 4% of the time, Pallas kernels for 0%

commit v1 on v0

--- a/solution.py
+++ b/solution.py
@@ -14,10 +14,9 @@
 EPSILON = 1e-06
 
 
-def partner(value, axis, distance):
-    mask = 2**distance
-    pairs = [(source, source ^ mask) for source in range(lax.axis_size(axis))]
-    return lax.ppermute(value, axis, pairs)
+def mirrored(value, axis):
+    last = lax.axis_size(axis) - 1
+    return lax.ppermute(value, axis, [(source, last - source) for source in range(last + 1)])
 
 
 def shifted(block, axis, distance):
@@ -123,23 +122,14 @@
     return (grad_q, key_value_gradient, jnp.stack([q_gain, k_gain]))
 
 
-def ascend(first, second, third, fourth, quantize_levels):
-    for bit_number in range(quantize_levels):
-        first, second, third, fourth = partner(
-            (first, second, third, fourth), "section", bit_number
-        )
-    return (first, second, third, fourth)
-
-
 def local(
     fresh_q, current_key_value, held_q, retained_key_value, cotangent, norm_gains, plan, segment_ids
 ):
-    quantize_levels = lax.axis_size("section").bit_length() - 1
     gain_per_row = norm_gains[0]
     id_table = segment_ids[0]
     forward_ids = lax.dynamic_index_in_dim(id_table, plan[0, 0], 0, keepdims=False)
     backward_ids = lax.dynamic_index_in_dim(id_table, plan[0, 1], 0, keepdims=False)
-    arrived = ascend(fresh_q, current_key_value, held_q, retained_key_value, quantize_levels)
+    arrived = mirrored((fresh_q, current_key_value, held_q, retained_key_value), "section")
     forward_out = forward(fresh_q[0], current_key_value[0], gain_per_row, forward_ids)
     attention_out = shifted(forward_out[None], "section", 1)
     upstream = shifted(cotangent, "section", -1)

time: 486 us -> 318 us (0.65)
  the two profiles are of different devices: /device:TPU:262 before, /device:TPU:1 now
where the time goes in v1:
time: 318 us; the launch traced here: 317 us
  blocking collectives  134 us (42%)
  waiting for transfers between devices  96.3 us (30%)
  starting transfers between devices  45.4 us (14%)
  local copies, waits for them, and re-layouts  17.8 us (6%)
  other arithmetic  11 us (3%)
  matrix products  7.41 us (2%)
  between operations  4.93 us (2%)
    psum x1, blocking collectives, local(): gain_total = lax.psum(gain_terms, 'dp') / lax.axis_size('dp')  134 us
    ppermute x4, waiting for transfers between devices, mirrored(): lax.ppermute(value, axis, [(source, last - source) for source in range(la...  96.3 us
    ppermute x4, starting transfers between devices, mirrored(): lax.ppermute(value, axis, [(source, last - source) for source in range(la...  34.2 us
    ppermute x2, starting transfers between devices, shifted(): return lax.ppermute(block, axis, route)  11.3 us
    unnamed x35, local copies, waits for them, and re-layouts  9.33 us
  transfers between devices with their start and end apart: 6, of which 2 were waited for; matrix products, arithmetic and copies ran while one was open for 9% of the time, Pallas kernels for 0%

profile of v1, /device:TPU:1, one launch (start us, length us, event | category | flops | bytes accessed | tf_op | source)
XLA Modules:
  0.0 317.0 jit_solution(3914469061671508701)
XLA Ops:
  0.6 20.9 %collective-permute-start.3 = (bf16[1,112,2048]{2,1,0:T(8,128)(2,1)}, bf16[1,112,2048]{2,1,0:T(8,128)(2,1)S(1)}, u32[]{:S(2)}, u32[]{:S(2)}) collective-permute-start(bf16[1,112,2048]{2,1,0:T(8,128)(2,1)} %param.10), channel_id=1, source_target_pairs={{0,960},{64,896},{128,832},{192,768},{256,704},{320,640},{384,576}... | collective-permute-start | bytes 1376264 | tf_op jit(solution)/shard_map/ppermute | solution.py:19
  21.6 1.9 collective-permute-start.4
  23.5 9.4 %collective-permute-start.5 = (bf16[1,112,2048]{2,1,0:T(8,128)(2,1)}, bf16[1,112,2048]{2,1,0:T(8,128)(2,1)}, u32[]{:S(2)}, u32[]{:S(2)}) collective-permute-start(bf16[1,112,2048]{2,1,0:T(8,128)(2,1)} %param.12), channel_id=1, source_target_pairs={{64,0},{128,64},{192,128},{256,192},{320,256},{384,320},{448,384},... | collective-permute-start | bytes 1376264 | tf_op jit(solution)/shard_map/ppermute | solution.py:25
  32.9 1.9 collective-permute-start.1
  34.8 9.4 %collective-permute-start.2 = (bf16[1,112,512]{2,1,0:T(8,128)(2,1)}, bf16[1,112,512]{2,1,0:T(8,128)(2,1)S(1)}, u32[]{:S(2)}, u32[]{:S(2)}) collective-permute-start(bf16[1,112,512]{2,1,0:T(8,128)(2,1)} %param.9), channel_id=1, source_target_pairs={{0,960},{64,896},{128,832},{192,768},{256,704},{320,640},{384,576}... | collective-permute-start | bytes 344072 | tf_op jit(solution)/shard_map/ppermute | solution.py:19
  44.2 1.3 fusion.52
  49.2 1.2 fusion.9
  51.8 0.7 dynamic-slice_bitcast_fusion
  52.5 0.7 fusion.40
  53.2 0.7 fusion.41
  55.6 0.6 copy-done.3
  57.4 1.0 convert_element_type.102
  59.6 77.1 %collective-permute-done.4 = bf16[1,112,512]{2,1,0:T(8,128)(2,1)} collective-permute-done((bf16[1,112,512]{2,1,0:T(8,128)(2,1)}, bf16[1,112,512]{2,1,0:T(8,128)(2,1)}, u32[]{:S(2)}, u32[]{:S(2)}) %collective-permute-start.4) | collective-permute-done | bytes 114720 | tf_op jit(solution)/shard_map/ppermute | solution.py:19
  136.7 1.9 collective-permute-start
  138.6 0.9 fusion.50
  139.9 19.1 %collective-permute-done.2 = bf16[1,112,512]{2,1,0:T(8,128)(2,1)S(1)} collective-permute-done((bf16[1,112,512]{2,1,0:T(8,128)(2,1)}, bf16[1,112,512]{2,1,0:T(8,128)(2,1)S(1)}, u32[]{:S(2)}, u32[]{:S(2)}) %collective-permute-start.2) | collective-permute-done | bytes 114720 | tf_op jit(solution)/shard_map/ppermute | solution.py:19
  160.3 1.1 copy.175
  162.1 1.5 fusion.2
  163.6 1.8 fusion.8
  165.5 1.7 multiply_reduce_fusion.1
  167.2 1.2 multiply_reduce_fusion
  168.5 0.7 copy-done.8
  169.1 1.4 fusion.28
  173.0 1.2 mul.295
  174.2 1.3 mul.296
  175.6 0.6 copy-done.12
  176.2 134.2 %psum.7 = f32[2,128]{1,0:T(2,128)S(1)} all-reduce(f32[2,128]{1,0:T(2,128)S(1)} %pad_maximum_fusion.1), channel_id=1, replica_groups=mesh['section'=16,'dp'=64] {'dp'}, use_global_device_ids=true, to_apply=%region_11.12 | all-reduce | flops 256 | bytes 2048 | tf_op jit(solution)/shard_map/psum | solution.py:139
  310.4 0.7 pad_maximum_fusion
  311.7 1.1 fusion.12
  312.7 1.8 copy.218
  314.5 1.8 copy.219
  316.4 0.6 copy.220
  (76 shorter events, 10.5 us)
Async XLA Ops:
  0.6 158.4 %collective-permute-start.3 = (bf16[1,112,2048]{2,1,0:T(8,128)(2,1)}, bf16[1,112,2048]{2,1,0:T(8,128)(2,1)S(1)}, u32[]{:S(2)}, u32[]{:S(2)}) collective-permute-start(bf16[1,112,2048]{2,1,0:T(8,128)(2,1)} %param.10), channel_id=1, source_target_pairs={{0,960},{64,896},{128,832},{192,768},{256,704},{320,640},{384,576}... | collective-permute-start | bytes 1376264 | tf_op jit(solution)/shard_map/ppermute | solution.py:19
  21.6 115.2 %collective-permute-start.4 = (bf16[1,112,512]{2,1,0:T(8,128)(2,1)}, bf16[1,112,512]{2,1,0:T(8,128)(2,1)}, u32[]{:S(2)}, u32[]{:S(2)}) collective-permute-start(bf16[1,112,512]{2,1,0:T(8,128)(2,1)} %param.11), channel_id=1, source_target_pairs={{0,960},{64,896},{128,832},{192,768},{256,704},{320,640},{384,576}... | collective-permute-start | bytes 344072 | tf_op jit(solution)/shard_map/ppermute | solution.py:19
  23.5 136.8 %collective-permute-start.5 = (bf16[1,112,2048]{2,1,0:T(8,128)(2,1)}, bf16[1,112,2048]{2,1,0:T(8,128)(2,1)}, u32[]{:S(2)}, u32[]{:S(2)}) collective-permute-start(bf16[1,112,2048]{2,1,0:T(8,128)(2,1)} %param.12), channel_id=1, source_target_pairs={{64,0},{128,64},{192,128},{256,192},{320,256},{384,320},{448,384},... | collective-permute-start | bytes 1376264 | tf_op jit(solution)/shard_map/ppermute | solution.py:25
  32.9 278.8 %collective-permute-start.1 = (bf16[1,112,2048]{2,1,0:T(8,128)(2,1)}, bf16[1,112,2048]{2,1,0:T(8,128)(2,1)}, u32[]{:S(2)}, u32[]{:S(2)}) collective-permute-start(bf16[1,112,2048]{2,1,0:T(8,128)(2,1)} %param.8), channel_id=1, source_target_pairs={{0,960},{64,896},{128,832},{192,768},{256,704},{320,640},{384,576}... | collective-permute-start | bytes 1376264 | tf_op jit(solution)/shard_map/ppermute | solution.py:19
  34.8 124.2 %collective-permute-start.2 = (bf16[1,112,512]{2,1,0:T(8,128)(2,1)}, bf16[1,112,512]{2,1,0:T(8,128)(2,1)S(1)}, u32[]{:S(2)}, u32[]{:S(2)}) collective-permute-start(bf16[1,112,512]{2,1,0:T(8,128)(2,1)} %param.9), channel_id=1, source_target_pairs={{0,960},{64,896},{128,832},{192,768},{256,704},{320,640},{384,576}... | collective-permute-start | bytes 344072 | tf_op jit(solution)/shard_map/ppermute | solution.py:19
  47.5 0.7 copy-start.11
  49.2 1.2 copy-start
  50.4 3.5 %copy-start.1 = (bf16[1,112,512]{2,1,0:T(8,128)(2,1)S(1)}, bf16[1,112,512]{2,1,0:T(8,128)(2,1)}, u32[]{:S(2)}) copy-start(bf16[1,112,512]{2,1,0:T(8,128)(2,1)} %param.9) | copy-start | bytes 344068
  55.6 0.7 copy-start.3
  55.6 0.7 copy-start.10
  55.6 0.7 copy-start.6
  55.6 0.7 copy-start.7
  58.4 0.6 copy-start.9
  136.7 38.8 %collective-permute-start = (bf16[1,112,2048]{2,1,0:T(8,128)(2,1)}, bf16[1,112,2048]{2,1,0:T(8,128)(2,1)}, u32[]{:S(2)}, u32[]{:S(2)}) collective-permute-start(bf16[1,112,2048]{2,1,0:T(8,128)(2,1)} %convert_element_type.102), channel_id=1, source_target_pairs={{960,0},{0,64},{64,128},{128,192},{192,256},{256,320},{320,384},{3... | collective-permute-start | bytes 1376264 | tf_op jit(solution)/shard_map/ppermute | solution.py:25
  161.4 0.7 copy-start.2
  168.5 0.7 copy-start.8
  172.2 0.7 copy-start.5
  175.6 0.7 copy-start.12
  175.6 0.7 copy-start.13
  310.4 1.2 copy-start.4

commit v2 on v1

v2 whole, which is shorter than its diff:
```python
import functools
import math

import jax
import jax.numpy as jnp
from jax import lax
from jax.experimental import pallas as pl
from jax.experimental.pallas import tpu as pltpu
from jax.sharding import PartitionSpec as P

F32, BF16 = jnp.float32, jnp.bfloat16
D = 128
HEADS, KV_HEADS = 16, 2
PER_KV = HEADS // KV_HEADS
GROUP = 4
EPSILON = 1e-06
SCALE = 1.0 / math.sqrt(D)
MESH = pl.DeviceIdType.MESH

HELD_KV, HELD_Q, COT, ATT, SIDE, GRAD_Q, GRAD_KV, GAIN, FRESH_KV, FRESH_Q = range(10)
CHUNKS = HEADS // GROUP
ROUND = FRESH_Q + CHUNKS

L_FQ, L_FKV, L_SIDE, L_HQ, L_HKV, L_COT, L_GQ, L_GKV, L_GAIN, L_ATT, L_CHUNK = range(11)


def dot(a, b, dims):
    return lax.dot_general(a, b, ((dims[:1], dims[1:]), ((), ())), preferred_element_type=F32)


def lane_sum(a):
    return jnp.sum(a, axis=-1, keepdims=True)


def fold(a):
    return jnp.sum(a.reshape(-1, 8, D), axis=0)


def head(i):
    start = i * D
    return pl.ds(start if isinstance(i, int) else pl.multiple_of(start, D), D)


def prepare(kv, side, slot, row, keys, values, mask):
    tokens = kv.shape[0]
    ids = jnp.broadcast_to(side[slot, row : row + 1, :], (D, D))
    rows = lax.broadcasted_iota(jnp.int32, (D, D), 0)
    cols = lax.broadcasted_iota(jnp.int32, (D, D), 1)
    allowed = jnp.where((ids == ids.T) & (cols <= rows), 1.0, 0.0)
    mask[...] = allowed[:tokens]
    gain = side[slot, 1:2, :]
    pad = jnp.zeros((D - tokens, D), BF16)
    for g in range(KV_HEADS):
        x = kv[:, head(g)].astype(F32)
        r = lax.rsqrt(jnp.mean(x * x, axis=-1, keepdims=True) + EPSILON)
        keys[g, :tokens, :] = (x * r * gain).astype(BF16)
        keys[g, tokens:, :] = pad
        values[g, :tokens, :] = kv[:, head(KV_HEADS + g)]
        values[g, tokens:, :] = pad


def probabilities(q, lanes, gain, k, mask):
    x = q[:, lanes].astype(F32)
    r = lax.rsqrt(jnp.mean(x * x, axis=-1, keepdims=True) + EPSILON)
    qn = (x * r * gain).astype(BF16)
    w = jnp.exp(dot(qn, k, (1, 1)) * SCALE) * mask[...]
    return x, r, qn, w * (1.0 / lane_sum(w))


def forward_step(it, q, side, slot, keys, values, mask, out):
    g = it // (PER_KV // GROUP)
    k, v = keys[g], values[g]
    gain = side[slot, 0:1, :]
    for u in range(GROUP):
        lanes = head(it * GROUP + u)
        p = probabilities(q, lanes, gain, k, mask)[3]
        out[:, lanes] = dot(p.astype(BF16), v, (1, 0)).astype(BF16)


def backward(q, kv, cot, side, slot, keys, values, mask, dk, dv, sums, grad_q, grad_kv):
    tokens = q.shape[0]
    prepare(kv, side, slot, 3, keys, values, mask)
    dk[...] = jnp.zeros_like(dk)
    dv[...] = jnp.zeros_like(dv)
    sums[...] = jnp.zeros_like(sums)

    @pl.loop(0, CHUNKS)
    def _(it):
        g = it // (PER_KV // GROUP)
        k, v = keys[g], values[g]
        gain = side[slot, 0:1, :]
        for u in range(GROUP):
            lanes = head(it * GROUP + u)
            x, r, qn, p = probabilities(q, lanes, gain, k, mask)
            up = cot[:, lanes]
            d_p = dot(up, v, (1, 1))
            dv[g] += dot(p.astype(BF16), up, (0, 0))
            d_s = (p * (d_p - lane_sum(p * d_p))).astype(BF16)
            d_qn = dot(d_s, k, (1, 0)) * SCALE
            dk[g] += dot(d_s, qn, (0, 0))
            scaled = gain * d_qn
            inner = lane_sum(x * scaled) * (1.0 / D)
            grad_q[:, lanes] = (r * scaled - x * (r * r * r * inner)).astype(BF16)
            sums[0] += fold(d_qn * x * r)

    gain = side[slot, 1:2, :]
    for g in range(KV_HEADS):
        x = kv[:, head(g)].astype(F32)
        r = lax.rsqrt(jnp.mean(x * x, axis=-1, keepdims=True) + EPSILON)
        d_kn = dk[g, :tokens, :] * SCALE
        scaled = gain * d_kn
        inner = lane_sum(x * scaled) * (1.0 / D)
        grad_kv[:, head(g)] = (r * scaled - x * (r * r * r * inner)).astype(BF16)
        grad_kv[:, head(KV_HEADS + g)] = dv[g, :tokens, :].astype(BF16)
        sums[1] += fold(d_kn * x * r)


def gain_rows(sums):
    q = jnp.sum(sums[0], axis=0, keepdims=True)
    k = jnp.sum(sums[1], axis=0, keepdims=True)
    row = lax.broadcasted_iota(jnp.int32, (8, D), 0)
    return jnp.where(row == 0, q, jnp.where(row == 1, k, 0.0))


def kernel(
    sections, replicas,
    fresh_q, fresh_kv, held_q, held_kv, cot, side,
    att_out, stored_q, stored_kv, grad_q_out, grad_kv_out, gain_out,
    q_vm, kv_vm, att_vm, hq_vm, hkv_vm, cot_vm, gq_vm, gkv_vm, side_vm,
    own_q, own_kv, own_cot, far_gq, far_gkv,
    keys, values, mask, dk, dv, sums, part, got, final,
    send, recv, local,
):
    s, d = lax.axis_index("section"), lax.axis_index("dp")
    mirror, up, down = sections - 1 - s, lax.rem(s + 1, sections), lax.rem(s + sections - 1, sections)
    rounds = replicas.bit_length() - 1
    partners = [d + (1 << i) * (1 - 2 * lax.rem(d // (1 << i), 2)) for i in range(rounds)]
    half = sections // 2
    giver = (s == half - 1) | (s == sections - 1)
    taker = (s == 0) | (s == half)
    normal = jnp.logical_not(giver | taker)

    def remote(src, dst, slot, section):
        return pltpu.make_async_remote_copy(
            src_ref=src, dst_ref=dst, send_sem=send.at[slot], recv_sem=recv.at[slot],
            device_id={"section": section}, device_id_type=MESH,
        )

    def chunk(ref, i):
        start = i * GROUP * D
        return ref.at[:, pl.ds(start if isinstance(i, int) else pl.multiple_of(start, GROUP * D), GROUP * D)]

    def load(src, dst, slot):
        return pltpu.make_async_copy(src, dst, local.at[slot])

    copy_held_kv = remote(held_kv.at[0], hkv_vm, HELD_KV, mirror)
    copy_held_q = remote(held_q.at[0], hq_vm, HELD_Q, mirror)
    copy_cot = remote(cot.at[0], cot_vm, COT, down)
    copy_att = remote(att_vm, att_out.at[0], ATT, up)
    copy_side = remote(side, side_vm.at[1], SIDE, mirror)
    copy_gq = remote(far_gq, grad_q_out.at[0], GRAD_Q, mirror)
    copy_gkv = remote(far_gkv, grad_kv_out.at[0], GRAD_KV, mirror)
    copy_gain = remote(final.at[1], gain_out, GAIN, mirror)
    copy_fresh_kv = remote(fresh_kv.at[0], stored_kv.at[0], FRESH_KV, mirror)

    def copy_fresh_q(i):
        return remote(chunk(fresh_q.at[0], i), chunk(stored_q.at[0], i), FRESH_Q + i, mirror)

    load_fq = load(fresh_q.at[0], q_vm, L_FQ)
    load_fkv = load(fresh_kv.at[0], kv_vm, L_FKV)
    load_side = load(side, side_vm.at[0], L_SIDE)
    load_hq = load(held_q.at[0], own_q, L_HQ)
    load_hkv = load(held_kv.at[0], own_kv, L_HKV)
    load_cot = load(cot.at[0], own_cot, L_COT)
    put_gq = load(gq_vm, grad_q_out.at[0], L_GQ)
    put_gkv = load(gkv_vm, grad_kv_out.at[0], L_GKV)
    put_gain = load(final.at[0], gain_out, L_GAIN)

    barrier = pltpu.get_barrier_semaphore()
    for section in (mirror, up, down):
        pl.semaphore_signal(barrier, inc=1, device_id={"section": section}, device_id_type=MESH)
    for partner in partners:
        pl.semaphore_signal(barrier, inc=1, device_id={"dp": partner}, device_id_type=MESH)

    load_side.start()

    @pl.when(jnp.logical_not(giver))
    def _():
        load_fkv.start()
        load_fq.start()

    @pl.when(taker)
    def _():
        load_hkv.start()
        load_hq.start()
        load_cot.start()

    pl.semaphore_wait(barrier, 3 + rounds)

    @pl.when(giver)
    def _():
        copy_side.start()

    @pl.when(jnp.logical_not(taker))
    def _():
        copy_cot.start()
        copy_held_kv.start()
        copy_held_q.start()

    @pl.when(jnp.logical_not(normal))
    def _():
        copy_fresh_kv.start()
        for i in range(CHUNKS):
            copy_fresh_q(i).start()

    load_side.wait()

    @pl.when(jnp.logical_not(giver))
    def _():
        load_fkv.wait()
        prepare(kv_vm, side_vm, 0, 2, keys, values, mask)
        load_fq.wait()

        @pl.loop(0, CHUNKS)
        def _(it):
            forward_step(it, q_vm, side_vm, 0, keys, values, mask, att_vm)

        copy_att.start()

    @pl.when(normal)
    def _():
        copy_fresh_kv.start()
        for i in range(CHUNKS):
            copy_fresh_q(i).start()

    @pl.when(taker)
    def _():
        load_hkv.wait()
        load_hq.wait()
        load_cot.wait()
        copy_side.wait_recv()
        backward(own_q, own_kv, own_cot, side_vm, 1, keys, values, mask, dk, dv, sums, far_gq, far_gkv)
        copy_gkv.start()
        copy_gq.start()
        part[0, 1] = gain_rows(sums)

    @pl.when(normal)
    def _():
        part[0, 1] = jnp.zeros((8, D), F32)

    @pl.when(jnp.logical_not(giver))
    def _():
        copy_cot.wait_recv()
        copy_held_kv.wait_recv()
        copy_held_q.wait_recv()
        backward(hq_vm, hkv_vm, cot_vm, side_vm, 0, keys, values, mask, dk, dv, sums, gq_vm, gkv_vm)
        put_gkv.start()
        put_gq.start()
        part[0, 0] = gain_rows(sums)

        for i, partner in enumerate(partners):
            exchange = pltpu.make_async_remote_copy(
                src_ref=part.at[i], dst_ref=got.at[i], send_sem=send.at[ROUND + i], recv_sem=recv.at[ROUND + i],
                device_id={"dp": partner}, device_id_type=MESH,
            )
            exchange.start()
            exchange.wait()
            if i < rounds - 1:
                part[i + 1] = part[i] + got[i]
            else:
                final[...] = (part[i] + got[i]) * (1.0 / replicas)
        put_gain.start()

    @pl.when(taker)
    def _():
        copy_gain.start()
        copy_fresh_kv.wait_recv()
        load_fkv2 = load(stored_kv.at[0], kv_vm, L_FKV)
        load_fkv2.start()
        load_fkv2.wait()
        prepare(kv_vm, side_vm, 1, 2, keys, values, mask)

        @pl.loop(0, CHUNKS)
        def _(it):
            copy_fresh_q(it).wait_recv()
            bring = load(chunk(stored_q.at[0], it), chunk(own_q, it), L_CHUNK)
            bring.start()
            bring.wait()
            forward_step(it, own_q, side_vm, 1, keys, values, mask, own_cot)
            load(chunk(own_cot, it), chunk(att_out.at[0], it), L_ATT).start()

        load(own_cot, att_out.at[0], L_ATT).wait()
        copy_gkv.wait_send()
        copy_gq.wait_send()
        copy_gain.wait_send()

    @pl.when(giver)
    def _():
        copy_side.wait_send()
        copy_gkv.wait_recv()
        copy_gq.wait_recv()
        copy_gain.wait_recv()

    @pl.when(jnp.logical_not(taker))
    def _():
        copy_cot.wait_send()
        copy_held_kv.wait_send()
        copy_held_q.wait_send()
        copy_att.wait_recv()
        copy_fresh_kv.wait_recv()
        for i in range(CHUNKS):
            copy_fresh_q(i).wait_recv()

    @pl.when(jnp.logical_not(giver))
    def _():
        copy_att.wait_send()
        put_gq.wait()
        put_gkv.wait()
        put_gain.wait()

    copy_fresh_kv.wait_send()
    for i in range(CHUNKS):
        copy_fresh_q(i).wait_send()


def local_tick(sections, replicas, fresh_q, fresh_kv, held_q, held_kv, cot, gains, plan, segment_ids):
    tokens, width, kv_width = fresh_q.shape[1], fresh_q.shape[2], fresh_kv.shape[2]
    ids = [lax.dynamic_slice_in_dim(segment_ids[0], plan[0, i], 1, 0).astype(F32) for i in range(2)]
    ids = jnp.pad(jnp.concatenate(ids, axis=0), ((0, 4), (0, D - tokens)))
    side = jnp.concatenate([gains[0], ids], axis=0)
    rounds = replicas.bit_length() - 1
    wide, narrow = (tokens, width), (tokens, kv_width)
    anywhere = pl.BlockSpec(memory_space=pl.ANY)
    shape = jax.ShapeDtypeStruct
    outs = pl.pallas_call(
        functools.partial(kernel, sections, replicas),
        out_shape=(
            shape((1, *wide), BF16), shape((1, *wide), BF16), shape((1, *narrow), BF16),
            shape((1, *wide), BF16), shape((1, *narrow), BF16), shape((8, D), F32),
        ),
        in_specs=[anywhere] * 6,
        out_specs=(anywhere,) * 6,
        scratch_shapes=[
            pltpu.VMEM(wide, BF16), pltpu.VMEM(narrow, BF16), pltpu.VMEM(wide, BF16),
            pltpu.VMEM(wide, BF16), pltpu.VMEM(narrow, BF16), pltpu.VMEM(wide, BF16),
            pltpu.VMEM(wide, BF16), pltpu.VMEM(narrow, BF16), pltpu.VMEM((2, 8, D), F32),
            pltpu.VMEM(wide, BF16), pltpu.VMEM(narrow, BF16), pltpu.VMEM(wide, BF16),
            pltpu.VMEM(wide, BF16), pltpu.VMEM(narrow, BF16),
            pltpu.VMEM((KV_HEADS, D, D), BF16), pltpu.VMEM((KV_HEADS, D, D), BF16),
            pltpu.VMEM((tokens, D), F32),
            pltpu.VMEM((KV_HEADS, D, D), F32), pltpu.VMEM((KV_HEADS, D, D), F32),
            pltpu.VMEM((2, 8, D), F32),
            pltpu.VMEM((rounds, 2, 8, D), F32), pltpu.VMEM((rounds, 2, 8, D), F32), pltpu.VMEM((2, 8, D), F32),
            pltpu.SemaphoreType.DMA((ROUND + rounds,)),
            pltpu.SemaphoreType.DMA((ROUND + rounds,)),
            pltpu.SemaphoreType.DMA((L_CHUNK + 1,)),
        ],
        compiler_params=pltpu.CompilerParams(collective_id=0, has_side_effects=True, vmem_limit_bytes=VMEM_LIMIT),
    )(fresh_q, fresh_kv, held_q, held_kv, cot, side)
    return (*outs[:5], outs[5][None, :2])


VMEM_LIMIT = 16 * 2**20


def solution(mesh):
    tokens = P("section", "dp", None)
    return jax.shard_map(
        functools.partial(local_tick, mesh.shape["section"], mesh.shape["dp"]),
        mesh=mesh,
        in_specs=(tokens,) * 5 + (P("section", None, None), P("section", None), P("dp", None, None)),
        out_specs=(tokens,) * 5 + (P("section", None, None),),
        check_vma=False,
    )
```

time: 318 us -> 156 us (0.49)
  Pallas kernels: 0 us -> 138 us
  blocking collectives: 134 us -> 0 us
  waiting for transfers between devices: 96.3 us -> 0 us
  starting transfers between devices: 45.4 us -> 0 us
  other arithmetic: 11 us -> 0.79 us
  matrix products: 7.41 us -> 0 us
  local copies, waits for them, and re-layouts: 17.8 us -> 10.9 us
    pallas_call x0 -> x1, Pallas kernels: none -> 138 us  [local_tick(): pl.pallas_call(functools.partial(kernel, sections, replicas), out_shape=(...]
    psum x1 -> x0, blocking collectives: 134 us -> none  [local(): gain_total = lax.psum(gain_terms, 'dp') / lax.axis_size('dp')]
    ppermute x6 -> x0, waiting for transfers between devices: 96.3 us -> none  [the longest x4 96.3 us: mirrored(): lax.ppermute(value, axis, [(source, last - source) for source in range(la...]
    ppermute x6 -> x0, starting transfers between devices: 45.4 us -> none  [the longest x4 34.2 us: mirrored(): lax.ppermute(value, axis, [(source, last - source) for source in range(la...]
    dot_general x7 -> x0, matrix products: 7.41 us -> none  [the longest x2 2.12 us: attention_probs(): jnp.einsum('qhgd,khd->hgqk', query_converted, k_cast, preferred_element_t...]
    mul x6 -> x0, local copies, waits for them, and re-layouts: 4.11 us -> none  [the longest x4 2.99 us: norm_back(): d_input = factor * scaled - widened * factor * factor * factor * inner]
    unnamed x35 -> x19, local copies, waits for them, and re-layouts: 9.33 us -> 9.76 us
  transfers between devices with their start and end apart: 6 -> 0, of which waited for: 2 -> 0; matrix products, arithmetic and copies ran while one was open for 9% -> 0% of each run, Pallas kernels for 0% -> 0%
where the time goes in v2:
time: 156 us; the launch traced here: 154 us
  Pallas kernels  138 us (88%)
  local copies, waits for them, and re-layouts  10.9 us (7%)
  between operations  4.54 us (3%)
    pallas_call x1, Pallas kernels, local_tick(): pl.pallas_call(functools.partial(kernel, sections, replicas), out_shape=(...  138 us
    unnamed x19, local copies, waits for them, and re-layouts  9.76 us

profile of v2, /device:TPU:1, one launch (start us, length us, event | category | flops | bytes accessed | tf_op | source)
XLA Modules:
  0.0 154.3 jit_solution(16365434257905041384)
XLA Ops:
  0.6 0.0 copy-start.5
  0.6 0.6 copy-done.5
  1.3 0.6 fusion
  5.8 0.8 convert_bitcast_fusion.1
  6.5 0.0 copy-start.6
  6.5 0.7 copy-done.6
  7.2 0.0 copy-start
  7.2 1.0 copy-done
  8.2 0.0 copy-start.1
  8.2 1.0 copy-done.1
  9.3 0.0 copy-start.2
  9.3 1.0 copy-done.2
  10.3 0.0 copy-start.3
  10.3 0.9 copy-done.3
  11.2 0.0 copy-start.4
  11.2 0.9 copy-done.4
  12.1 138.1 %shard_map.127 = (bf16[1,112,2048]{2,1,0:T(8,128)(2,1)S(1)}, bf16[1,112,2048]{2,1,0:T(8,128)(2,1)S(1)}, bf16[1,112,512]{2,1,0:T(8,128)(2,1)S(1)}, bf16[1,112,204...) custom-call(bf16[1,112,2048]{2,1,0:T(8,128)(2,1)S(1)} %copy-done, ...), custom_call_target="tpu_custom_call" | custom-call | tf_op jit(solution)/shard_map/pallas_call | solution.py:335
  150.2 0.6 slice_bitcast_fusion
  150.7 0.8 copy.19
  151.5 0.8 copy.20
  152.3 0.6 copy.21
  152.9 0.8 copy.22
  153.7 0.6 copy.23
  (2 shorter events, 0.0 us)
Async XLA Ops:
  0.6 0.7 copy-start.5
  6.5 0.7 copy-start.6
  7.2 1.0 copy-start
  8.2 1.0 copy-start.1
  9.3 1.0 copy-start.2
  10.3 0.9 copy-start.3
  11.2 0.9 copy-start.4

commit v3 on v2

--- a/solution.py
+++ b/solution.py
@@ -12,6 +12,7 @@
 D = 128
 HEADS, KV_HEADS = 16, 2
 PER_KV = HEADS // KV_HEADS
+PLACES = 4
 GROUP = 4
 EPSILON = 1e-06
 SCALE = 1.0 / math.sqrt(D)
@@ -21,7 +22,7 @@
 CHUNKS = HEADS // GROUP
 ROUND = FRESH_Q + CHUNKS
 
-L_FQ, L_FKV, L_SIDE, L_HQ, L_HKV, L_COT, L_GQ, L_GKV, L_GAIN, L_ATT, L_CHUNK = range(11)
+L_FQ, L_FKV, L_GAINS, L_SEGMENTS, L_PLAN, L_HQ, L_HKV, L_COT, L_GQ, L_GKV, L_GAIN, L_ATT, L_CHUNK = range(13)
 
 
 def dot(a, b, dims):
@@ -124,18 +125,25 @@
 
 def kernel(
     sections, replicas,
-    fresh_q, fresh_kv, held_q, held_kv, cot, side,
+    fresh_q, fresh_kv, held_q, held_kv, cot, gains, plan, segments,
     att_out, stored_q, stored_kv, grad_q_out, grad_kv_out, gain_out,
     q_vm, kv_vm, att_vm, hq_vm, hkv_vm, cot_vm, gq_vm, gkv_vm, side_vm,
     own_q, own_kv, own_cot, far_gq, far_gkv,
-    keys, values, mask, dk, dv, sums, part, got, final,
-    send, recv, local,
+    keys, values, mask, dk, dv, sums, part, got, final, gains_vm, segments_vm, plan_sm,
+    send, recv, local, gate,
 ):
     s, d = lax.axis_index("section"), lax.axis_index("dp")
     mirror, up, down = sections - 1 - s, lax.rem(s + 1, sections), lax.rem(s + sections - 1, sections)
     rounds = replicas.bit_length() - 1
     partners = [d + (1 << i) * (1 - 2 * lax.rem(d // (1 << i), 2)) for i in range(rounds)]
     half = sections // 2
+    stride = replicas // PLACES
+    z = d // stride
+    odd = lax.rem(s // (sections // 4), 2)
+    place = z + odd * (PLACES - 1 - 2 * z)
+    step = stride * (1 - 2 * odd)
+    farther = lax.rem(d + step + replicas, replicas)
+    nearer = lax.rem(d - step + replicas, replicas)
     giver = (s == half - 1) | (s == sections - 1)
     taker = (s == 0) | (s == half)
     normal = jnp.logical_not(giver | taker)
@@ -157,10 +165,10 @@
     copy_held_q = remote(held_q.at[0], hq_vm, HELD_Q, mirror)
     copy_cot = remote(cot.at[0], cot_vm, COT, down)
     copy_att = remote(att_vm, att_out.at[0], ATT, up)
-    copy_side = remote(side, side_vm.at[1], SIDE, mirror)
+    copy_side = remote(side_vm.at[0], side_vm.at[1], SIDE, mirror)
     copy_gq = remote(far_gq, grad_q_out.at[0], GRAD_Q, mirror)
     copy_gkv = remote(far_gkv, grad_kv_out.at[0], GRAD_KV, mirror)
-    copy_gain = remote(final.at[1], gain_out, GAIN, mirror)
+    copy_gain = remote(final.at[1], gain_out.at[0], GAIN, mirror)
     copy_fresh_kv = remote(fresh_kv.at[0], stored_kv.at[0], FRESH_KV, mirror)
 
     def copy_fresh_q(i):
@@ -168,21 +176,41 @@
 
     load_fq = load(fresh_q.at[0], q_vm, L_FQ)
     load_fkv = load(fresh_kv.at[0], kv_vm, L_FKV)
-    load_side = load(side, side_vm.at[0], L_SIDE)
+    load_gains = load(gains.at[0], gains_vm, L_GAINS)
+    load_plan = load(plan, plan_sm, L_PLAN)
+    load_segments = load(segments.at[0], segments_vm, L_SEGMENTS)
     load_hq = load(held_q.at[0], own_q, L_HQ)
     load_hkv = load(held_kv.at[0], own_kv, L_HKV)
     load_cot = load(cot.at[0], own_cot, L_COT)
     put_gq = load(gq_vm, grad_q_out.at[0], L_GQ)
     put_gkv = load(gkv_vm, grad_kv_out.at[0], L_GKV)
-    put_gain = load(final.at[0], gain_out, L_GAIN)
+    put_gain = load(final.at[0], gain_out.at[0], L_GAIN)
+
+    def first_is_out(copies):
+        for copy in copies:
+            copy.wait_send()
+
+        @pl.when(place > 0)
+        def _():
+            pl.semaphore_signal(gate, inc=1, device_id={"dp": nearer}, device_id_type=MESH)
+
+    def wait_for_turn():
+        @pl.when(place < PLACES - 1)
+        def _():
+            pl.semaphore_wait(gate, 1)
+
+    fresh_copies = [copy_fresh_kv, *(copy_fresh_q(i) for i in range(CHUNKS))]
+    held_copies = [copy_held_kv, copy_held_q]
 
     barrier = pltpu.get_barrier_semaphore()
     for section in (mirror, up, down):
         pl.semaphore_signal(barrier, inc=1, device_id={"section": section}, device_id_type=MESH)
-    for partner in partners:
+    for partner in (*partners, farther, nearer):
         pl.semaphore_signal(barrier, inc=1, device_id={"dp": partner}, device_id_type=MESH)
 
-    load_side.start()
+    load_plan.start()
+    load_gains.start()
+    load_segments.start()
 
     @pl.when(jnp.logical_not(giver))
     def _():
@@ -195,7 +223,17 @@
         load_hq.start()
         load_cot.start()
 
-    pl.semaphore_wait(barrier, 3 + rounds)
+    load_plan.wait()
+    load_gains.wait()
+    load_segments.wait()
+    side_vm[0] = jnp.zeros((8, D), F32)
+    side_vm[0, 0:2, :] = gains_vm[...]
+    micro = lax.broadcasted_iota(jnp.int32, segments_vm.shape, 0)
+    for i in range(2):
+        row = jnp.sum(jnp.where(micro == plan_sm[0, i], segments_vm[...], 0), axis=0, keepdims=True)
+        side_vm[0, 2 + i : 3 + i, : segments_vm.shape[1]] = row.astype(F32)
+
+    pl.semaphore_wait(barrier, 5 + rounds)
 
     @pl.when(giver)
     def _():
@@ -207,13 +245,10 @@
         copy_held_kv.start()
         copy_held_q.start()
 
-    @pl.when(jnp.logical_not(normal))
-    def _():
-        copy_fresh_kv.start()
-        for i in range(CHUNKS):
-            copy_fresh_q(i).start()
-
-    load_side.wait()
+    @pl.when(taker)
+    def _():
+        for copy in fresh_copies:
+            copy.start()
 
     @pl.when(jnp.logical_not(giver))
     def _():
@@ -227,11 +262,12 @@
 
         copy_att.start()
 
-    @pl.when(normal)
-    def _():
-        copy_fresh_kv.start()
-        for i in range(CHUNKS):
-            copy_fresh_q(i).start()
+    @pl.when(jnp.logical_not(taker))
+    def _():
+        wait_for_turn()
+        for copy in fresh_copies:
+            copy.start()
+        first_is_out(held_copies)
 
     @pl.when(taker)
     def _():
@@ -240,8 +276,10 @@
         load_cot.wait()
         copy_side.wait_recv()
         backward(own_q, own_kv, own_cot, side_vm, 1, keys, values, mask, dk, dv, sums, far_gq, far_gkv)
+        wait_for_turn()
         copy_gkv.start()
         copy_gq.start()
+        first_is_out(fresh_copies)
         part[0, 1] = gain_rows(sums)
 
     @pl.when(normal)
@@ -268,7 +306,7 @@
             if i < rounds - 1:
                 part[i + 1] = part[i] + got[i]
             else:
-                final[...] = (part[i] + got[i]) * (1.0 / replicas)
+                final[...] = ((part[i] + got[i]) * (1.0 / replicas))[:, :2]
         put_gain.start()
 
     @pl.when(taker)
@@ -304,12 +342,10 @@
     @pl.when(jnp.logical_not(taker))
     def _():
         copy_cot.wait_send()
-        copy_held_kv.wait_send()
-        copy_held_q.wait_send()
         copy_att.wait_recv()
-        copy_fresh_kv.wait_recv()
-        for i in range(CHUNKS):
-            copy_fresh_q(i).wait_recv()
+        for copy in fresh_copies:
+            copy.wait_send()
+            copy.wait_recv()
 
     @pl.when(jnp.logical_not(giver))
     def _():
@@ -318,27 +354,34 @@
         put_gkv.wait()
         put_gain.wait()
 
-    copy_fresh_kv.wait_send()
-    for i in range(CHUNKS):
-        copy_fresh_q(i).wait_send()
+
+def in_hbm(x):
+    return pltpu.with_memory_space_constraint(x, pltpu.HBM)
+
+
+def finish(*refs):
+    half = len(refs) // 2
+    copies = [pltpu.make_async_copy(refs[i], refs[half + i], refs[-1].at[i]) for i in range(half)]
+    for copy in copies:
+        copy.start()
+    for copy in copies:
+        copy.wait()
 
 
 def local_tick(sections, replicas, fresh_q, fresh_kv, held_q, held_kv, cot, gains, plan, segment_ids):
     tokens, width, kv_width = fresh_q.shape[1], fresh_q.shape[2], fresh_kv.shape[2]
-    ids = [lax.dynamic_slice_in_dim(segment_ids[0], plan[0, i], 1, 0).astype(F32) for i in range(2)]
-    ids = jnp.pad(jnp.concatenate(ids, axis=0), ((0, 4), (0, D - tokens)))
-    side = jnp.concatenate([gains[0], ids], axis=0)
     rounds = replicas.bit_length() - 1
     wide, narrow = (tokens, width), (tokens, kv_width)
-    anywhere = pl.BlockSpec(memory_space=pl.ANY)
+    anywhere, hbm = pl.BlockSpec(memory_space=pl.ANY), pl.BlockSpec(memory_space=pltpu.HBM)
     shape = jax.ShapeDtypeStruct
+    out_shape = (
+        shape((1, *wide), BF16), shape((1, *wide), BF16), shape((1, *narrow), BF16),
+        shape((1, *wide), BF16), shape((1, *narrow), BF16), shape((1, 2, D), F32),
+    )
     outs = pl.pallas_call(
         functools.partial(kernel, sections, replicas),
-        out_shape=(
-            shape((1, *wide), BF16), shape((1, *wide), BF16), shape((1, *narrow), BF16),
-            shape((1, *wide), BF16), shape((1, *narrow), BF16), shape((8, D), F32),
-        ),
-        in_specs=[anywhere] * 6,
+        out_shape=out_shape,
+        in_specs=[hbm] * 8,
         out_specs=(anywhere,) * 6,
         scratch_shapes=[
             pltpu.VMEM(wide, BF16), pltpu.VMEM(narrow, BF16), pltpu.VMEM(wide, BF16),
@@ -350,14 +393,23 @@
             pltpu.VMEM((tokens, D), F32),
             pltpu.VMEM((KV_HEADS, D, D), F32), pltpu.VMEM((KV_HEADS, D, D), F32),
             pltpu.VMEM((2, 8, D), F32),
-            pltpu.VMEM((rounds, 2, 8, D), F32), pltpu.VMEM((rounds, 2, 8, D), F32), pltpu.VMEM((2, 8, D), F32),
+            pltpu.VMEM((rounds, 2, 8, D), F32), pltpu.VMEM((rounds, 2, 8, D), F32), pltpu.VMEM((2, 2, D), F32),
+            pltpu.VMEM((2, D), F32), pltpu.VMEM(segment_ids.shape[1:], jnp.int32), pltpu.SMEM((1, 2), jnp.int32),
             pltpu.SemaphoreType.DMA((ROUND + rounds,)),
             pltpu.SemaphoreType.DMA((ROUND + rounds,)),
             pltpu.SemaphoreType.DMA((L_CHUNK + 1,)),
+            pltpu.SemaphoreType.REGULAR,
         ],
         compiler_params=pltpu.CompilerParams(collective_id=0, has_side_effects=True, vmem_limit_bytes=VMEM_LIMIT),
-    )(fresh_q, fresh_kv, held_q, held_kv, cot, side)
-    return (*outs[:5], outs[5][None, :2])
+    )(*(in_hbm(x) for x in (fresh_q, fresh_kv, held_q, held_kv, cot, gains, plan, segment_ids)))
+    return pl.pallas_call(
+        finish,
+        out_shape=out_shape,
+        in_specs=[anywhere] * 6,
+        out_specs=(hbm,) * 6,
+        scratch_shapes=[pltpu.SemaphoreType.DMA((6,))],
+        compiler_params=pltpu.CompilerParams(vmem_limit_bytes=2**20),
+    )(*outs)
 
 
 VMEM_LIMIT = 16 * 2**20

time: 156 us -> 142 us (0.910)
  local copies, waits for them, and re-layouts: 10.9 us -> 0 us
  between operations: 4.54 us -> 0.64 us
    unnamed x19 -> x0, local copies, waits for them, and re-layouts: 9.76 us -> none
    pallas_call x1 -> x2, Pallas kernels: 138 us -> 139 us  [the longest x1 138 us: local_tick(): pl.pallas_call(functools.partial(kernel, sections, replicas), out_shape=o...]
where the time goes in v3:
time: 142 us; the launch traced here: 140 us
  Pallas kernels  139 us (98%)
    pallas_call x1, Pallas kernels, local_tick(): pl.pallas_call(functools.partial(kernel, sections, replicas), out_shape=o...  138 us

profile of v3, /device:TPU:1, one launch (start us, length us, event | category | flops | bytes accessed | tf_op | source)
XLA Modules:
  0.0 139.5 jit_solution(13911888087468698250)
XLA Ops:
  0.6 137.7 %shard_map.127 = (bf16[1,112,2048]{2,1,0:T(8,128)(2,1)S(1)}, bf16[1,112,2048]{2,1,0:T(8,128)(2,1)S(1)}, bf16[1,112,512]{2,1,0:T(8,128)(2,1)S(1)}, bf16[1,112,204...) custom-call(bf16[1,112,2048]{2,1,0:T(8,128)(2,1)} %fresh_q.1, ...), custom_call_target="tpu_custom_call" | custom-call | tf_op jit(solution)/shard_map/pallas_call | solution.py:381
  138.3 1.2 shard_map.128

commit v4 on v3

--- a/solution.py
+++ b/solution.py
@@ -117,10 +117,7 @@
 
 
 def gain_rows(sums):
-    q = jnp.sum(sums[0], axis=0, keepdims=True)
-    k = jnp.sum(sums[1], axis=0, keepdims=True)
-    row = lax.broadcasted_iota(jnp.int32, (8, D), 0)
-    return jnp.where(row == 0, q, jnp.where(row == 1, k, 0.0))
+    return jnp.concatenate([jnp.sum(sums[i], axis=0, keepdims=True) for i in range(2)], axis=0)
 
 
 def kernel(
@@ -139,11 +136,11 @@
     half = sections // 2
     stride = replicas // PLACES
     z = d // stride
-    odd = lax.rem(s // (sections // 4), 2)
-    place = z + odd * (PLACES - 1 - 2 * z)
-    step = stride * (1 - 2 * odd)
-    farther = lax.rem(d + step + replicas, replicas)
-    nearer = lax.rem(d - step + replicas, replicas)
+    even = 1 - lax.rem(s // (sections // 4), 2)
+    place = z + even * (PLACES - 1 - 2 * z)
+    step = stride * (1 - 2 * even)
+    later = lax.rem(d + step + replicas, replicas)
+    earlier = lax.rem(d - step + replicas, replicas)
     giver = (s == half - 1) | (s == sections - 1)
     taker = (s == 0) | (s == half)
     normal = jnp.logical_not(giver | taker)
@@ -192,7 +189,7 @@
 
         @pl.when(place > 0)
         def _():
-            pl.semaphore_signal(gate, inc=1, device_id={"dp": nearer}, device_id_type=MESH)
+            pl.semaphore_signal(gate, inc=1, device_id={"dp": earlier}, device_id_type=MESH)
 
     def wait_for_turn():
         @pl.when(place < PLACES - 1)
@@ -205,7 +202,7 @@
     barrier = pltpu.get_barrier_semaphore()
     for section in (mirror, up, down):
         pl.semaphore_signal(barrier, inc=1, device_id={"section": section}, device_id_type=MESH)
-    for partner in (*partners, farther, nearer):
+    for partner in (*partners, later, earlier):
         pl.semaphore_signal(barrier, inc=1, device_id={"dp": partner}, device_id_type=MESH)
 
     load_plan.start()
@@ -284,7 +281,7 @@
 
     @pl.when(normal)
     def _():
-        part[0, 1] = jnp.zeros((8, D), F32)
+        part[0, 1] = jnp.zeros((2, D), F32)
 
     @pl.when(jnp.logical_not(giver))
     def _():
@@ -306,7 +303,7 @@
             if i < rounds - 1:
                 part[i + 1] = part[i] + got[i]
             else:
-                final[...] = ((part[i] + got[i]) * (1.0 / replicas))[:, :2]
+                final[...] = (part[i] + got[i]) * (1.0 / replicas)
         put_gain.start()
 
     @pl.when(taker)
@@ -393,7 +390,7 @@
             pltpu.VMEM((tokens, D), F32),
             pltpu.VMEM((KV_HEADS, D, D), F32), pltpu.VMEM((KV_HEADS, D, D), F32),
             pltpu.VMEM((2, 8, D), F32),
-            pltpu.VMEM((rounds, 2, 8, D), F32), pltpu.VMEM((rounds, 2, 8, D), F32), pltpu.VMEM((2, 2, D), F32),
+            pltpu.VMEM((rounds, 2, 2, D), F32), pltpu.VMEM((rounds, 2, 2, D), F32), pltpu.VMEM((2, 2, D), F32),
             pltpu.VMEM((2, D), F32), pltpu.VMEM(segment_ids.shape[1:], jnp.int32), pltpu.SMEM((1, 2), jnp.int32),
             pltpu.SemaphoreType.DMA((ROUND + rounds,)),
             pltpu.SemaphoreType.DMA((ROUND + rounds,)),

time: 142 us -> 127 us (0.89)
  the two profiles are of different devices: /device:TPU:1 before, /device:TPU:215 now
where the time goes in v4:
time: 127 us
  Pallas kernels  126 us (99%)
    pallas_call x1, Pallas kernels, local_tick(): pl.pallas_call(functools.partial(kernel, sections, replicas), out_shape=o...  125 us

profile of v4, /device:TPU:215, one launch (start us, length us, event | category | flops | bytes accessed | tf_op | source)
XLA Modules:
  0.0 126.6 jit_solution(10582042030955195134)
XLA Ops:
  0.6 124.8 %shard_map.127 = (bf16[1,112,2048]{2,1,0:T(8,128)(2,1)S(1)}, bf16[1,112,2048]{2,1,0:T(8,128)(2,1)S(1)}, bf16[1,112,512]{2,1,0:T(8,128)(2,1)S(1)}, bf16[1,112,204...) custom-call(bf16[1,112,2048]{2,1,0:T(8,128)(2,1)} %fresh_q.1, ...), custom_call_target="tpu_custom_call" | custom-call | tf_op jit(solution)/shard_map/pallas_call | solution.py:378
  125.4 1.2 shard_map.128

commit v5 on v4

--- a/solution.py
+++ b/solution.py
@@ -12,6 +12,7 @@
 D = 128
 HEADS, KV_HEADS = 16, 2
 PER_KV = HEADS // KV_HEADS
+CORES = 2
 PLACES = 4
 GROUP = 4
 EPSILON = 1e-06
@@ -126,17 +127,22 @@
     att_out, stored_q, stored_kv, grad_q_out, grad_kv_out, gain_out,
     q_vm, kv_vm, att_vm, hq_vm, hkv_vm, cot_vm, gq_vm, gkv_vm, side_vm,
     own_q, own_kv, own_cot, far_gq, far_gkv,
-    keys, values, mask, dk, dv, sums, part, got, final, gains_vm, segments_vm, plan_sm,
+    keys, values, mask, dk, dv, sums, part, around, final, gains_vm, segments_vm, plan_sm,
     send, recv, local, gate,
 ):
     s, d = lax.axis_index("section"), lax.axis_index("dp")
     mirror, up, down = sections - 1 - s, lax.rem(s + 1, sections), lax.rem(s + sections - 1, sections)
-    rounds = replicas.bit_length() - 1
-    partners = [d + (1 << i) * (1 - 2 * lax.rem(d // (1 << i), 2)) for i in range(rounds)]
     half = sections // 2
     stride = replicas // PLACES
     z = d // stride
     even = 1 - lax.rem(s // (sections // 4), 2)
+    ring = replicas // PLACES // CORES
+    core, y = lax.rem(d, CORES), lax.rem(d // CORES, ring)
+    other = d + 1 - 2 * core
+    right = d + CORES * (lax.rem(y + 1, ring) - y)
+    left = d + CORES * (lax.rem(y + ring - 1, ring) - y)
+    pair = d + stride * (1 - 2 * lax.rem(z, 2))
+    middle = (z > 0) & (z < PLACES - 1)
     place = z + even * (PLACES - 1 - 2 * z)
     step = stride * (1 - 2 * even)
     later = lax.rem(d + step + replicas, replicas)
@@ -183,10 +189,7 @@
     put_gkv = load(gkv_vm, grad_kv_out.at[0], L_GKV)
     put_gain = load(final.at[0], gain_out.at[0], L_GAIN)
 
-    def first_is_out(copies):
-        for copy in copies:
-            copy.wait_send()
-
+    def free_the_earlier():
         @pl.when(place > 0)
         def _():
             pl.semaphore_signal(gate, inc=1, device_id={"dp": earlier}, device_id_type=MESH)
@@ -202,8 +205,16 @@
     barrier = pltpu.get_barrier_semaphore()
     for section in (mirror, up, down):
         pl.semaphore_signal(barrier, inc=1, device_id={"section": section}, device_id_type=MESH)
-    for partner in (*partners, later, earlier):
+    for partner in (other, right, left):
         pl.semaphore_signal(barrier, inc=1, device_id={"dp": partner}, device_id_type=MESH)
+
+    @pl.when(z > 0)
+    def _():
+        pl.semaphore_signal(barrier, inc=1, device_id={"dp": d - stride}, device_id_type=MESH)
+
+    @pl.when(z < PLACES - 1)
+    def _():
+        pl.semaphore_signal(barrier, inc=1, device_id={"dp": d + stride}, device_id_type=MESH)
 
     load_plan.start()
     load_gains.start()
@@ -230,17 +241,22 @@
         row = jnp.sum(jnp.where(micro == plan_sm[0, i], segments_vm[...], 0), axis=0, keepdims=True)
         side_vm[0, 2 + i : 3 + i, : segments_vm.shape[1]] = row.astype(F32)
 
-    pl.semaphore_wait(barrier, 5 + rounds)
+    pl.semaphore_wait(barrier, 6 + jnp.where(z > 0, 1, 0) + jnp.where(z < PLACES - 1, 1, 0))
 
     @pl.when(giver)
     def _():
         copy_side.start()
 
+    waiting = (s == sections - sections // 4) & (place < PLACES // 2)
+
     @pl.when(jnp.logical_not(taker))
     def _():
+        for copy in held_copies:
+            copy.start()
+
+    @pl.when(jnp.logical_not(taker | waiting))
+    def _():
         copy_cot.start()
-        copy_held_kv.start()
-        copy_held_q.start()
 
     @pl.when(taker)
     def _():
@@ -261,10 +277,22 @@
 
     @pl.when(jnp.logical_not(taker))
     def _():
+        @pl.when(waiting)
+        def _():
+            for copy in held_copies:
+                copy.wait_send()
+            copy_cot.start()
+
         wait_for_turn()
         for copy in fresh_copies:
             copy.start()
-        first_is_out(held_copies)
+
+        @pl.when(jnp.logical_not(waiting))
+        def _():
+            for copy in held_copies:
+                copy.wait_send()
+
+        free_the_earlier()
 
     @pl.when(taker)
     def _():
@@ -276,7 +304,9 @@
         wait_for_turn()
         copy_gkv.start()
         copy_gq.start()
-        first_is_out(fresh_copies)
+        for copy in fresh_copies:
+            copy.wait_send()
+        free_the_earlier()
         part[0, 1] = gain_rows(sums)
 
     @pl.when(normal)
@@ -293,17 +323,60 @@
         put_gq.start()
         part[0, 0] = gain_rows(sums)
 
-        for i, partner in enumerate(partners):
-            exchange = pltpu.make_async_remote_copy(
-                src_ref=part.at[i], dst_ref=got.at[i], send_sem=send.at[ROUND + i], recv_sem=recv.at[ROUND + i],
-                device_id={"dp": partner}, device_id_type=MESH,
+        def along_dp(src, dst, slot, device):
+            return pltpu.make_async_remote_copy(
+                src_ref=src, dst_ref=dst, send_sem=send.at[ROUND + slot], recv_sem=recv.at[ROUND + slot],
+                device_id={"dp": device}, device_id_type=MESH,
             )
-            exchange.start()
-            exchange.wait()
-            if i < rounds - 1:
-                part[i + 1] = part[i] + got[i]
-            else:
-                final[...] = (part[i] + got[i]) * (1.0 / replicas)
+
+        cores = along_dp(part.at[0], part.at[1], 0, other)
+        cores.start()
+        cores.wait()
+        around[y] = part[0] + part[1]
+        sent = []
+        for k in range(ring // 2):
+            block = around.at[lax.rem(y + ring - k, ring)]
+            steps = [along_dp(block, block, 1 + k, right)]
+            if k < ring // 2 - 1:
+                block = around.at[lax.rem(y + k, ring)]
+                steps.append(along_dp(block, block, 1 + ring // 2 + k, left))
+            for step_copy in steps:
+                step_copy.start()
+            for step_copy in steps:
+                step_copy.wait_recv()
+            sent += steps
+        total = around[0]
+        for k in range(1, ring):
+            total += around[k]
+        if PLACES == 1:
+            final[...] = total * (1.0 / replicas)
+        else:
+            part[2] = total
+            first = along_dp(part.at[2], part.at[3], ring, pair)
+            first.start()
+            first.wait_recv()
+            second = along_dp(part.at[4], part.at[5], ring + 1, jnp.where(z == 1, d + stride, d - stride))
+            third = along_dp(part.at[6], part.at[7], ring + 2, pair)
+
+            @pl.when(middle)
+            def _():
+                part[4] = part[2] + part[3]
+                second.start()
+                second.wait_recv()
+                part[6] = part[4] + part[5]
+                third.start()
+                final[...] = part[6] * (1.0 / replicas)
+                second.wait_send()
+                third.wait_send()
+
+            @pl.when(jnp.logical_not(middle))
+            def _():
+                third.wait_recv()
+                final[...] = part[7] * (1.0 / replicas)
+
+            sent.append(first)
+        for step_copy in sent:
+            step_copy.wait_send()
         put_gain.start()
 
     @pl.when(taker)
@@ -367,7 +440,7 @@
 
 def local_tick(sections, replicas, fresh_q, fresh_kv, held_q, held_kv, cot, gains, plan, segment_ids):
     tokens, width, kv_width = fresh_q.shape[1], fresh_q.shape[2], fresh_kv.shape[2]
-    rounds = replicas.bit_length() - 1
+    ring = replicas // PLACES // CORES
     wide, narrow = (tokens, width), (tokens, kv_width)
     anywhere, hbm = pl.BlockSpec(memory_space=pl.ANY), pl.BlockSpec(memory_space=pltpu.HBM)
     shape = jax.ShapeDtypeStruct
@@ -390,10 +463,10 @@
             pltpu.VMEM((tokens, D), F32),
             pltpu.VMEM((KV_HEADS, D, D), F32), pltpu.VMEM((KV_HEADS, D, D), F32),
             pltpu.VMEM((2, 8, D), F32),
-            pltpu.VMEM((rounds, 2, 2, D), F32), pltpu.VMEM((rounds, 2, 2, D), F32), pltpu.VMEM((2, 2, D), F32),
+            pltpu.VMEM((8, 2, 2, D), F32), pltpu.VMEM((ring, 2, 2, D), F32), pltpu.VMEM((2, 2, D), F32),
             pltpu.VMEM((2, D), F32), pltpu.VMEM(segment_ids.shape[1:], jnp.int32), pltpu.SMEM((1, 2), jnp.int32),
-            pltpu.SemaphoreType.DMA((ROUND + rounds,)),
-            pltpu.SemaphoreType.DMA((ROUND + rounds,)),
+            pltpu.SemaphoreType.DMA((ROUND + ring + 3,)),
+            pltpu.SemaphoreType.DMA((ROUND + ring + 3,)),
             pltpu.SemaphoreType.DMA((L_CHUNK + 1,)),
             pltpu.SemaphoreType.REGULAR,
         ],

time: 127 us -> 123 us (0.969)
  the two profiles are of different devices: /device:TPU:215 before, /device:TPU:1 now
where the time goes in v5:
time: 123 us; the launch traced here: 120 us
  Pallas kernels  120 us (98%)
    pallas_call x1, Pallas kernels, local_tick(): pl.pallas_call(functools.partial(kernel, sections, replicas), out_shape=o...  119 us

profile of v5, /device:TPU:1, one launch (start us, length us, event | category | flops | bytes accessed | tf_op | source)
XLA Modules:
  0.0 120.4 jit_solution(16243218567561215732)
XLA Ops:
  0.6 118.6 %shard_map.127 = (bf16[1,112,2048]{2,1,0:T(8,128)(2,1)S(1)}, bf16[1,112,2048]{2,1,0:T(8,128)(2,1)S(1)}, bf16[1,112,512]{2,1,0:T(8,128)(2,1)S(1)}, bf16[1,112,204...) custom-call(bf16[1,112,2048]{2,1,0:T(8,128)(2,1)} %fresh_q.1, ...), custom_call_target="tpu_custom_call" | custom-call | tf_op jit(solution)/shard_map/pallas_call | solution.py:451
  119.2 1.2 shard_map.128

commit v6 on v5

--- a/solution.py
+++ b/solution.py
@@ -247,7 +247,7 @@
     def _():
         copy_side.start()
 
-    waiting = (s == sections - sections // 4) & (place < PLACES // 2)
+    waiting = (lax.rem(s, sections // 4) == 0) & (place < jnp.where(s == sections - sections // 4, PLACES // 2, 1))
 
     @pl.when(jnp.logical_not(taker))
     def _():

time: 123 us -> 123 us (level)
  no operation moved by 1% of the time
where the time goes in v6:
time: 123 us; the launch traced here: 120 us
  Pallas kernels  120 us (98%)
    pallas_call x1, Pallas kernels, local_tick(): pl.pallas_call(functools.partial(kernel, sections, replicas), out_shape=o...  119 us

profile of v6, /device:TPU:1, one launch (start us, length us, event | category | flops | bytes accessed | tf_op | source)
XLA Modules:
  0.0 120.4 jit_solution(4270961934798319556)
XLA Ops:
  0.6 118.6 %shard_map.127 = (bf16[1,112,2048]{2,1,0:T(8,128)(2,1)S(1)}, bf16[1,112,2048]{2,1,0:T(8,128)(2,1)S(1)}, bf16[1,112,512]{2,1,0:T(8,128)(2,1)S(1)}, bf16[1,112,204...) custom-call(bf16[1,112,2048]{2,1,0:T(8,128)(2,1)} %fresh_q.1, ...), custom_call_target="tpu_custom_call" | custom-call | tf_op jit(solution)/shard_map/pallas_call | solution.py:451
  119.2 1.2 shard_map.128
